TPU v7x, 32 devices: a whole 2x2x4 slice. The times are simulated.
32 devices in a mesh: dp: 4 (over y, x), fsdp: 4 (over z), crop: 2 (over core).
Axes of the slice: x: 2, y: 2, z: 4, core: 2. Of those that a mesh axis runs over, the one named last changes fastest.
Arguments:
- grad_parts: float32 [8, 848, 1536], P(('dp', 'crop'), None, 'fsdp'), may hold values from -1.5 to 1.5
- student: float32 [848, 1536], P(('dp', 'crop'), 'fsdp'), may hold values from -2 to 2
- teacher: float32 [848, 1536], P(('dp', 'crop'), 'fsdp'), may hold values from -2 to 2
- moment1: float32 [848, 1536], P(('dp', 'crop'), 'fsdp'), may hold values from -0.6 to 0.6
- moment2: float32 [848, 1536], P(('dp', 'crop'), 'fsdp'), may hold values from 0.001 to 0.01
- step_count: int32 [1], replicated, may hold values from 1 to 1999
- pixels: bfloat16 [16, 2, 256, 588], P(('dp', 'fsdp'), 'crop'), may hold values from -5 to 5
- assign: int32 [16, 2], P(('dp', 'fsdp')), may hold values from 0 to 1, each once within a row
Outputs:
- student_new: float32 [848, 1536], P(('dp', 'crop'), 'fsdp')
- moment1_new: float32 [848, 1536], P(('dp', 'crop'), 'fsdp')
- moment2_new: float32 [848, 1536], P(('dp', 'crop'), 'fsdp')
- teacher_new: float32 [848, 1536], P(('dp', 'crop'), 'fsdp')
- student_step: float32 [848, 1536], P(('dp', 'crop'), 'fsdp')
- teacher_tokens: float32 [16, 2, 257, 1536], P(('dp', 'fsdp'))
Inputs may be any that keep to these rules, and one draw needn't show every extreme that they name: `assign`: each row holds 0 and 1 once.
All inputs are finite; a program needn't handle non-finite values.
Results may differ from a plain program's by a relative error of at most 0.0003.
Values may be sent and summed in bfloat16 or wider, within the bound.
A program may use at most 64 MiB of HBM per device.

v0:
```python
import math
import jax
import jax.numpy as jnp
from jax import lax
from jax.sharding import PartitionSpec as P

beta_one = 0.9
beta_two = 0.999
adam_epsilon = 1e-08
learn_rate = 0.001
weight_decay = 0.04
momentum_base = 0.992
plan_length = 625000.0
norm_epsilon = 1e-06


def optimize(gradient, student, teacher, moment1, moment2, step_count):
    step_value = step_count[0].astype(jnp.float32)
    first_moment = beta_one * moment1 + (1.0 - beta_one) * gradient
    second_moment = beta_two * moment2 + (1.0 - beta_two) * gradient * gradient
    first_fix = 1.0 - jnp.power(jnp.float32(beta_one), step_value)
    second_fix = 1.0 - jnp.power(jnp.float32(beta_two), step_value)
    update = (
        first_moment / first_fix / (jnp.sqrt(second_moment / second_fix) + adam_epsilon)
        + weight_decay * student
    )
    student_new = student - learn_rate * update
    momentum = (
        1.0 - (1.0 - momentum_base) * (jnp.cos(math.pi * step_value / plan_length) + 1.0) / 2.0
    )
    teacher_new = momentum * teacher + (1.0 - momentum) * student_new
    return (student_new, first_moment, second_moment, teacher_new, update)


def embed(patches, table):
    count = patches.shape[0]
    pix_size = patches.shape[2]
    patch_count = patches.shape[1]
    width = table.shape[1]
    weight = table[:pix_size]
    position = table[pix_size : pix_size + patch_count]
    extras = table[pix_size + patch_count :]
    flat_patches = patches.reshape(count * patch_count, pix_size).astype(jnp.float32)
    projected = jnp.dot(
        flat_patches, weight, precision=lax.Precision.HIGHEST, preferred_element_type=jnp.float32
    )
    projected = projected.reshape(count, patch_count, width) + extras[1] + position
    class_row = jnp.broadcast_to(extras[0], (count, 1, width))
    tokens = jnp.concatenate([class_row, projected], axis=1)
    average = jnp.mean(tokens, axis=-1, keepdims=True)
    centered = tokens - average
    variance = jnp.mean(centered * centered, axis=-1, keepdims=True)
    return centered * lax.rsqrt(variance + norm_epsilon) * extras[2] + extras[3]


def shards(grad_parts, student, teacher, moment1, moment2, step_count, pixels, assign):
    gradient = lax.psum_scatter(grad_parts[0], ("dp", "crop"), scatter_dimension=0, tiled=True)
    student_new, first_moment, second_moment, teacher_new, update = optimize(
        gradient, student, teacher, moment1, moment2, step_count
    )
    column_block = lax.all_gather(teacher_new, "fsdp", axis=1, tiled=True)
    gathered = lax.all_gather(column_block, ("dp", "crop"), axis=0, tiled=True)
    own_tokens = embed(pixels[:, 0], gathered)
    both = lax.all_gather(own_tokens[:, None], "crop", axis=1, tiled=True)
    teacher_tokens = jnp.where((assign == 0)[:, :, None, None], both[:, 0:1], both[:, 1:2])
    return (student_new, first_moment, second_moment, teacher_new, update, teacher_tokens)


def solution(mesh):
    placed = (
        P(("dp", "crop"), None, "fsdp"),
        P(("dp", "crop"), "fsdp"),
        P(("dp", "crop"), "fsdp"),
        P(("dp", "crop"), "fsdp"),
        P(("dp", "crop"), "fsdp"),
        P(),
        P(("dp", "fsdp"), "crop", None, None),
        P(("dp", "fsdp"), None),
    )
    return jax.shard_map(
        shards,
        mesh=mesh,
        in_specs=placed,
        out_specs=(
            P(("dp", "crop"), "fsdp"),
            P(("dp", "crop"), "fsdp"),
            P(("dp", "crop"), "fsdp"),
            P(("dp", "crop"), "fsdp"),
            P(("dp", "crop"), "fsdp"),
            P(("dp", "fsdp"), None, None, None),
        ),
        check_vma=False,
    )
```

profile of v0, /device:TPU:0, one launch (start us, length us, event | category | flops | bytes accessed | tf_op | source)
XLA Modules:
  0.0 138.0 jit_solution(8425231990737697508)
XLA Ops:
  7.2 0.0 copy-start
  7.2 0.0 copy-start.6
  7.2 0.0 all-gather.6.cloned.1.call-start
  7.3 23.7 %fusion = f32[112,384]{1,0:T(8,128)S(1)} fusion(f32[848,384]{1,0:T(8,128)} %bitcast.31), kind=kCustom, calls=%all-reduce-scatter | all-reduce-scatter fusion | flops 344065 | bytes 1475072
  31.0 1.3 collective-permute-start
  33.2 0.6 dynamic-slice.4
  34.4 0.3 concatenate.29
  34.7 0.9 multiply_add_fusion
  35.7 19.0 %all_gather.9 = f32[106,1536]{1,0:T(8,128)} all-gather(f32[106,384]{1,0:T(8,128)S(1)} %get-tuple-element.9), channel_id=1, replica_groups=mesh['dp'=4,'fsdp'=4,'crop'=2] {'fsdp'}, dimensions={1}, use_global_device_ids=true | all-gather | bytes 814080 | tf_op jit(solution)/shard_map/all_gather | solution.py:61
  54.6 0.0 all-gather.6.cloned.1.call-update
  54.7 0.0 all-gather.4.cloned.1.call-start
  54.7 42.3 %all-gather.6.cloned.1.call-done = f32[8,106,1536]{2,1,0:T(8,128)} async-done(((f32[1,106,1536]{2,1,0:T(8,128)}), f32[8,106,1536]{2,1,0:T(8,128)}) %all-gather.6.cloned.1.call-update) | async-done | bytes 5210128 | tf_op jit(solution)/shard_map/all_gather | solution.py:62
  97.0 4.5 %reshape.278 = f32[848,1536]{1,0:T(8,128)} reshape(f32[8,106,1536]{2,1,0:T(8,128)} %all-gather.6.cloned.1.call-done) | data formatting | bytes 10420224
  101.5 1.0 slice_reduce_fusion.1
  102.5 4.9 %fusion.9 = f32[256,1536]{1,0:T(8,128)S(1)} fusion(f32[848,1536]{1,0:T(8,128)} %reshape.278, f32[1536]{0:T(1024)S(1)} %get-tuple-element.8, bf16[1,1,256,588]{2,3,1,0:T(8,128)(2,1)S(1)} %copy-done), kind=kOutput, calls=%fused_computation.5 | convolution fusion | flops 2775318528 | bytes 7090176 | tf_op jit(solution)/shard_map/dot_general | solution.py:44
  107.4 0.3 fusion.15
  107.7 0.5 multiply_reduce_fusion
  108.1 0.4 fusion.14
  108.5 2.8 %copy.14 = f32[1,1,257,1536]{3,0,2,1:T(1,128)} copy(f32[1,1,257,1536]{3,2,1,0:T(8,128)S(1)} %fusion.14) | data formatting | bytes 3158016 | tf_op jit(solution)/shard_map/add | solution.py:53
  111.3 0.0 all-gather.4.cloned.1.call-update
  111.3 12.3 %all-gather.4.cloned.1.call-done = f32[1,2,257,1536]{3,0,2,1:T(1,128)} async-done(((f32[1,1,257,1536]{3,0,2,1:T(1,128)}), f32[1,2,257,1536]{3,0,2,1:T(1,128)}) %all-gather.4.cloned.1.call-update) | async-done | bytes 3158032 | tf_op jit(solution)/shard_map/all_gather | solution.py:64
  123.6 4.0 %fusion.19 = (f32[1,1,257,1536]{3,0,2,1:T(1,128)S(1)}, f32[1,1,257,1536]{3,0,2,1:T(1,128)S(1)}) fusion(f32[1,2,257,1536]{3,0,2,1:T(1,128)} %all-gather.4.cloned.1.call-done), kind=kLoop, calls=%fused_computation.30 | loop fusion | bytes 6316032 | tf_op jit(solution)/shard_map/slice | solution.py:65
  127.7 0.2 copy_bitcast_fusion
  127.9 3.2 %broadcast_select_fusion = f32[1,2,257,1536]{3,1,2,0:T(2,128)} fusion(pred[2]{0:T(512)(128)(4,1)S(1)} %compare_bitcast_fusion, f32[257,1536]{1,0:T(8,128)S(1)} %get-tuple-element.18, f32[257,1536]{1,0:T(8,128)S(1)} %get-tuple-element.19), kind=kLoop, calls=%fused_computation.2 | loop fusion | flops 789504 | bytes 6316034 | tf_op jit(solution)/shard_map/jit(_where)/select_n | solution.py:65
  (19 shorter events, 0.1 us)
Async XLA Ops:
  7.2 95.4 %copy-start = (bf16[1,1,256,588]{2,3,1,0:T(8,128)(2,1)S(1)}, bf16[1,1,256,588]{2,3,1,0:T(8,128)(2,1)}, u32[]{:S(2)}) copy-start(bf16[1,1,256,588]{2,3,1,0:T(8,128)(2,1)} %param.14) | copy-start | bytes 903172
  7.2 26.0 %copy-start.6 = (u32[32]{0:T(128)S(1)}, u32[32]{0:T(128)}, u32[]{:S(2)}) copy-start(u32[32]{0:T(128)} %constant.56) | copy-start | bytes 388
  7.2 27.5 %copy-start.2 = (f32[106,384]{1,0:T(8,128)S(1)}, f32[106,384]{1,0:T(8,128)}, u32[]{:S(2)}) copy-start(f32[106,384]{1,0:T(8,128)} %param.10) | copy-start | bytes 488452
  7.2 27.5 %copy-start.5 = (f32[106,384]{1,0:T(8,128)S(1)}, f32[106,384]{1,0:T(8,128)}, u32[]{:S(2)}) copy-start(f32[106,384]{1,0:T(8,128)} %param.11) | copy-start | bytes 488452
  7.2 27.5 %copy-start.4 = (f32[106,384]{1,0:T(8,128)S(1)}, f32[106,384]{1,0:T(8,128)}, u32[]{:S(2)}) copy-start(f32[106,384]{1,0:T(8,128)} %param.12) | copy-start | bytes 488452
  7.2 27.5 %copy-start.3 = (f32[106,384]{1,0:T(8,128)S(1)}, f32[106,384]{1,0:T(8,128)}, u32[]{:S(2)}) copy-start(f32[106,384]{1,0:T(8,128)} %param.9) | copy-start | bytes 488452
  7.2 89.8 %all-gather.6.cloned.1.call-start = ((), (), s32[]{:S(2)}) async-start(), calls=%async_computation.1 | async-start | bytes 6193152 | tf_op jit(solution)/shard_map/all_gather | solution.py:62
  31.0 3.4 %collective-permute-start = (f32[42,384]{1,0:T(8,128)S(1)}, f32[42,384]{1,0:T(8,128)S(1)}, u32[]{:S(2)}, u32[]{:S(2)}) collective-permute-start(f32[42,384]{1,0:T(8,128)S(1)} %slice.45), channel_id=1, source_target_pairs={{0,1},{1,8},{8,9},{9,16},{16,17},{17,24},{24,25},{2,3},{3,10},{10,... | collective-permute-start | bytes 193544
  35.7 65.8 %copy-start.1 = (f32[106,384]{1,0:T(8,128)}, f32[106,384]{1,0:T(8,128)S(1)}, u32[]{:S(2)}) copy-start(f32[106,384]{1,0:T(8,128)S(1)} %get-tuple-element.9) | copy-start | bytes 488452
  54.7 68.9 %all-gather.4.cloned.1.call-start = ((), (), s32[]{:S(2)}) async-start(), calls=%async_computation | async-start | bytes 4737024 | tf_op jit(solution)/shard_map/all_gather | solution.py:64
  108.5 2.8 %copy-start.7 = (s32[1,2]{1,0:T(1,128)S(1)}, s32[1,2]{1,0:T(1,128)}, u32[]{:S(2)}) copy-start(s32[1,2]{1,0:T(1,128)} %param.15) | copy-start | bytes 28
Sparse Core Ops, SparseCore 0:
  54.8 42.1 all-gather.5
  111.4 12.1 all-gather.3
where the time goes:
time: 138 us
  waiting for transfers between devices  54.6 us (40%)
  blocking collectives  42.7 us (31%)
  between operations  15.7 us (11%)
  local copies, waits for them, and re-layouts  13.4 us (10%)
  other arithmetic  5.28 us (4%)
  matrix products  4.87 us (4%)
    all_gather x1, waiting for transfers between devices, shards(): gathered = lax.all_gather(column_block, ('dp', 'crop'), axis=0, tiled=True)  42.3 us
    unnamed x1, blocking collectives  23.7 us
    all_gather x1, blocking collectives, shards(): column_block = lax.all_gather(teacher_new, 'fsdp', axis=1, tiled=True)  19 us
    all_gather x1, waiting for transfers between devices, shards(): both = lax.all_gather(own_tokens[:, None], 'crop', axis=1, tiled=True)  12.3 us
    unnamed x21, local copies, waits for them, and re-layouts  5.6 us
    dot_general x1, matrix products, embed(): jnp.dot(flat_patches, weight, precision=lax.Precision.HIGHEST, preferred_...  4.87 us
    slice x1, local copies, waits for them, and re-layouts, shards(): both[:, 0:1]  4.05 us
    select_n x1, other arithmetic, shards(): jnp.where((assign == 0)[:, :, None, None], both[:, 0:1], both[:, 1:2])  3.22 us
  transfers between devices with their start and end apart: 3, of which 2 were waited for; matrix products, arithmetic and copies ran while one was open for 0% of the time, Pallas kernels for 0%

commit v1 on v0

--- a/solution.py
+++ b/solution.py
@@ -61,7 +61,10 @@
     column_block = lax.all_gather(teacher_new, "fsdp", axis=1, tiled=True)
     gathered = lax.all_gather(column_block, ("dp", "crop"), axis=0, tiled=True)
     own_tokens = embed(pixels[:, 0], gathered)
-    both = lax.all_gather(own_tokens[:, None], "crop", axis=1, tiled=True)
+    both = jnp.concatenate(
+        lax.all_to_all(jnp.stack([own_tokens[:, None]] * lax.axis_size("crop")), "crop", 0, 0),
+        axis=1,
+    )
     teacher_tokens = jnp.where((assign == 0)[:, :, None, None], both[:, 0:1], both[:, 1:2])
     return (student_new, first_moment, second_moment, teacher_new, update, teacher_tokens)
 

time: 138 us -> 131 us (0.949)
  waiting for transfers between devices: 54.6 us -> 42.4 us
  blocking collectives: 42.7 us -> 48.9 us
  local copies, waits for them, and re-layouts: 13.4 us -> 12 us
    all_gather x1 -> x0, waiting for transfers between devices: 12.3 us -> none  [shards(): both = lax.all_gather(own_tokens[:, None], 'crop', axis=1, tiled=True)]
    all_to_all x0 -> x1, blocking collectives: none -> 6.24 us  [shards(): lax.all_to_all(jnp.stack([own_tokens[:, None]] * lax.axis_size('crop')),...]
    another operation x0 -> x1, local copies, waits for them, and re-layouts: none -> 3.25 us  [shards(): jnp.stack([own_tokens[:, None]] * lax.axis_size('crop'))]
    add x1 -> x0, local copies, waits for them, and re-layouts: 2.77 us -> none  [embed(): return centered * lax.rsqrt(variance + norm_epsilon) * extras[2] + extras[3]]
    slice x1, local copies, waits for them, and re-layouts: 4.05 us -> 2.16 us  [shards(): both[:, 0:1]]
  transfers between devices with their start and end apart: 3 -> 2, of which waited for: 2 -> 1; matrix products, arithmetic and copies ran while one was open for 0% -> 0% of each run, Pallas kernels for 0% -> 0%
where the time goes in v1:
time: 131 us
  blocking collectives  48.9 us (37%)
  waiting for transfers between devices  42.4 us (32%)
  between operations  15.7 us (12%)
  local copies, waits for them, and re-layouts  12 us (9%)
  other arithmetic  5.67 us (4%)
  matrix products  4.87 us (4%)
  starting transfers between devices  1.33 us (1%)
    all_gather x1, waiting for transfers between devices, shards(): gathered = lax.all_gather(column_block, ('dp', 'crop'), axis=0, tiled=True)  42.3 us
    unnamed x1, blocking collectives  23.7 us
    all_gather x1, blocking collectives, shards(): column_block = lax.all_gather(teacher_new, 'fsdp', axis=1, tiled=True)  19 us
    all_to_all x1, blocking collectives, shards(): lax.all_to_all(jnp.stack([own_tokens[:, None]] * lax.axis_size('crop')),...  6.24 us
    unnamed x21, local copies, waits for them, and re-layouts  5.59 us
    dot_general x1, matrix products, embed(): jnp.dot(flat_patches, weight, precision=lax.Precision.HIGHEST, preferred_...  4.87 us
    another operation x1, local copies, waits for them, and re-layouts, shards(): jnp.stack([own_tokens[:, None]] * lax.axis_size('crop'))  3.25 us
    select_n x1, other arithmetic, shards(): jnp.where((assign == 0)[:, :, None, None], both[:, 0:1], both[:, 1:2])  3.22 us
  transfers between devices with their start and end apart: 2, of which 1 were waited for; matrix products, arithmetic and copies ran while one was open for 0% of the time, Pallas kernels for 0%

profile of v1, /device:TPU:0, one launch (start us, length us, event | category | flops | bytes accessed | tf_op | source)
XLA Modules:
  0.0 130.9 jit_solution(597426820782526132)
XLA Ops:
  7.2 0.0 copy-start
  7.2 0.0 copy-start.6
  7.2 0.0 all-gather.3.cloned.1.call-start
  7.3 23.7 %fusion = f32[112,384]{1,0:T(8,128)S(1)} fusion(f32[848,384]{1,0:T(8,128)} %bitcast.33), kind=kCustom, calls=%all-reduce-scatter | all-reduce-scatter fusion | flops 344065 | bytes 1475072
  31.0 1.3 collective-permute-start
  33.2 0.6 dynamic-slice.4
  34.4 0.3 concatenate.29
  34.7 0.0 copy-start.7
  34.8 0.9 multiply_add_fusion
  35.7 19.0 %all_gather.6 = f32[106,1536]{1,0:T(8,128)} all-gather(f32[106,384]{1,0:T(8,128)S(1)} %get-tuple-element.9), channel_id=1, replica_groups=mesh['dp'=4,'fsdp'=4,'crop'=2] {'fsdp'}, dimensions={1}, use_global_device_ids=true | all-gather | bytes 814080 | tf_op jit(solution)/shard_map/all_gather | solution.py:61
  54.7 0.0 all-gather.3.cloned.1.call-update
  54.7 42.3 %all-gather.3.cloned.1.call-done = f32[8,106,1536]{2,1,0:T(8,128)} async-done(((f32[1,106,1536]{2,1,0:T(8,128)}), f32[8,106,1536]{2,1,0:T(8,128)}) %all-gather.3.cloned.1.call-update) | async-done | bytes 5210128 | tf_op jit(solution)/shard_map/all_gather | solution.py:62
  97.0 4.5 %reshape.282 = f32[848,1536]{1,0:T(8,128)} reshape(f32[8,106,1536]{2,1,0:T(8,128)} %all-gather.3.cloned.1.call-done) | data formatting | bytes 10420224
  101.5 1.0 slice_reduce_fusion.1
  102.5 4.9 %fusion.9 = f32[256,1536]{1,0:T(8,128)S(1)} fusion(f32[848,1536]{1,0:T(8,128)} %reshape.282, f32[1536]{0:T(1024)S(1)} %get-tuple-element.8, bf16[1,1,256,588]{2,3,1,0:T(8,128)(2,1)S(1)} %copy-done), kind=kOutput, calls=%fused_computation.6 | convolution fusion | flops 2775318528 | bytes 7090176 | tf_op jit(solution)/shard_map/dot_general | solution.py:44
  107.4 0.3 fusion.15
  107.7 0.5 multiply_reduce_fusion
  108.1 0.4 fusion.14
  108.5 0.4 pad_maximum_fusion
  108.9 3.2 %copy.14 = f32[2,1,1,257,1536]{4,2,3,1,0:T(1,128)S(1)} copy(f32[2,1,1,257,1536]{4,3,2,1,0:T(8,128)S(1)} %pad_maximum_fusion) | data formatting | bytes 6316032 | tf_op jit(solution)/shard_map/stack | solution.py:65
  112.2 6.2 %all_to_all.5 = f32[2,1,1,257,1536]{4,2,3,1,0:T(1,128)S(1)} all-to-all(f32[2,1,1,257,1536]{4,2,3,1,0:T(1,128)S(1)} %copy.14), channel_id=1, replica_groups=mesh['dp'=4,'fsdp'=4,'crop'=2] {'crop'}, dimensions={0} | all-to-all | bytes 6316032 | tf_op jit(solution)/shard_map/all_to_all | solution.py:65
  118.4 2.2 %fusion.19 = (f32[1,1,257,1536]{3,0,2,1:T(1,128)S(1)}, f32[1,1,257,1536]{3,0,2,1:T(1,128)S(1)}) fusion(f32[1,2,257,1536]{3,0,2,1:T(1,128)S(1)} %bitcast.31), kind=kLoop, calls=%fused_computation.31 | loop fusion | bytes 6316032 | tf_op jit(solution)/shard_map/slice | solution.py:68
  120.6 0.2 copy_bitcast_fusion
  120.8 3.2 %broadcast_select_fusion = f32[1,2,257,1536]{3,1,2,0:T(2,128)} fusion(pred[2]{0:T(512)(128)(4,1)S(1)} %compare_bitcast_fusion, f32[257,1536]{1,0:T(8,128)S(1)} %get-tuple-element.18, f32[257,1536]{1,0:T(8,128)S(1)} %get-tuple-element.19), kind=kLoop, calls=%fused_computation.3 | loop fusion | flops 789504 | bytes 6316034 | tf_op jit(solution)/shard_map/jit(_where)/select_n | solution.py:68
  (18 shorter events, 0.1 us)
Async XLA Ops:
  7.2 95.4 %copy-start = (bf16[1,1,256,588]{2,3,1,0:T(8,128)(2,1)S(1)}, bf16[1,1,256,588]{2,3,1,0:T(8,128)(2,1)}, u32[]{:S(2)}) copy-start(bf16[1,1,256,588]{2,3,1,0:T(8,128)(2,1)} %param.14) | copy-start | bytes 903172
  7.2 26.0 %copy-start.6 = (u32[32]{0:T(128)S(1)}, u32[32]{0:T(128)}, u32[]{:S(2)}) copy-start(u32[32]{0:T(128)} %constant.56) | copy-start | bytes 388
  7.2 27.5 %copy-start.2 = (f32[106,384]{1,0:T(8,128)S(1)}, f32[106,384]{1,0:T(8,128)}, u32[]{:S(2)}) copy-start(f32[106,384]{1,0:T(8,128)} %param.10) | copy-start | bytes 488452
  7.2 27.5 %copy-start.5 = (f32[106,384]{1,0:T(8,128)S(1)}, f32[106,384]{1,0:T(8,128)}, u32[]{:S(2)}) copy-start(f32[106,384]{1,0:T(8,128)} %param.11) | copy-start | bytes 488452
  7.2 27.5 %copy-start.4 = (f32[106,384]{1,0:T(8,128)S(1)}, f32[106,384]{1,0:T(8,128)}, u32[]{:S(2)}) copy-start(f32[106,384]{1,0:T(8,128)} %param.12) | copy-start | bytes 488452
  7.2 27.5 %copy-start.3 = (f32[106,384]{1,0:T(8,128)S(1)}, f32[106,384]{1,0:T(8,128)}, u32[]{:S(2)}) copy-start(f32[106,384]{1,0:T(8,128)} %param.9) | copy-start | bytes 488452
  7.2 89.8 %all-gather.3.cloned.1.call-start = ((), (), s32[]{:S(2)}) async-start(), calls=%async_computation.1 | async-start | bytes 6193152 | tf_op jit(solution)/shard_map/all_gather | solution.py:62
  31.0 3.4 %collective-permute-start = (f32[42,384]{1,0:T(8,128)S(1)}, f32[42,384]{1,0:T(8,128)S(1)}, u32[]{:S(2)}, u32[]{:S(2)}) collective-permute-start(f32[42,384]{1,0:T(8,128)S(1)} %slice.45), channel_id=1, source_target_pairs={{0,1},{1,8},{8,9},{9,16},{16,17},{17,24},{24,25},{2,3},{3,10},{10,... | collective-permute-start | bytes 193544
  34.7 19.9 %copy-start.7 = (s32[1,2]{1,0:T(1,128)S(1)}, s32[1,2]{1,0:T(1,128)}, u32[]{:S(2)}) copy-start(s32[1,2]{1,0:T(1,128)} %param.15) | copy-start | bytes 28
  35.7 65.8 %copy-start.1 = (f32[106,384]{1,0:T(8,128)}, f32[106,384]{1,0:T(8,128)S(1)}, u32[]{:S(2)}) copy-start(f32[106,384]{1,0:T(8,128)S(1)} %get-tuple-element.9) | copy-start | bytes 488452
Sparse Core Ops, SparseCore 0:
  54.8 42.1 all-gather.2
